TPU v7x, 32 devices: a whole 2x2x4 slice. The times are simulated.
32 devices in a mesh: dp: 8 (over z, y), mp: 4 (over x, core).
Axes of the slice: x: 2, y: 2, z: 4, core: 2. Of those that a mesh axis runs over, the one named last changes fastest.
Arguments:
- tokens: bfloat16 [8192, 2048], P('dp'), may hold values from -6 to 6
- documents: int32 [8, 1024], P('dp'), may hold values from 0 to 3, never falling along the last dimension, each value on 1 to 512 neighbouring positions
- cotangent: bfloat16 [8192, 2048], P('dp'), may hold values from -6 to 6
- attn_gain: float32 [2048], P('dp'), may hold values from 0.5 to 1.5
- query_gain: float32 [128], P('dp'), may hold values from 1 to 2
- key_norm_scale: float32 [128], P('dp'), may hold values from 0.25 to 1.75
- query_weight: float32 [2048, 2048], P('dp', 'mp'), may hold values from -0.125 to 0.125
- key_projection: float32 [2048, 1024], P('dp', 'mp'), may hold values from -0.125 to 0.125
- value_projection: float32 [2048, 1024], P('dp', 'mp'), may hold values from -0.125 to 0.125
- output_weight: float32 [2048, 2048], P('mp', 'dp'), may hold values from -1 to 1
- mlp_gain: float32 [2048], P('dp'), may hold values from 0.5 to 1.5
- gate_weight: float32 [2048, 6144], P('dp', 'mp'), may hold values from -0.125 to 0.125
- up_weight: float32 [2048, 6144], P('dp', 'mp'), may hold values from -0.125 to 0.125
- down_weight: float32 [6144, 2048], P('mp', 'dp'), may hold values from -0.078125 to 0.078125
Outputs:
- layer_output: bfloat16 [8192, 2048], P(('dp', 'mp'))
- input_grad: float32 [8192, 2048], P(('dp', 'mp'))
- attn_gain_grad: float32 [2048], P('dp')
- query_gain_grad: float32 [128], P('dp')
- key_gain_grad: float32 [128], P('dp')
- query_weight_grad: float32 [2048, 2048], P('dp', 'mp')
- key_weight_grad: float32 [2048, 1024], P('dp', 'mp')
- value_weight_grad: float32 [2048, 1024], P('dp', 'mp')
- output_weight_grad: float32 [2048, 2048], P('mp', 'dp')
- mlp_gain_grad: float32 [2048], P('dp')
- gate_weight_grad: float32 [2048, 6144], P('dp', 'mp')
- up_weight_grad: float32 [2048, 6144], P('dp', 'mp')
- down_weight_grad: float32 [6144, 2048], P('mp', 'dp')
Inputs may be any that keep to these rules, and one draw needn't show every extreme that they name: `documents`: document numbers never fall along a sequence; each document holds 1 to 512 positions, and some document holds exactly 512.
All inputs are finite; a program needn't handle non-finite values.
Results may differ from a plain program's by a relative error of at most 0.023.
Values may be sent and summed in bfloat16 or wider, within the bound.
A program may use at most 256 MiB of HBM per device.

v0:
```python
import jax
import jax.numpy as jnp
from jax import lax
from jax.sharding import PartitionSpec as P

QUERY_HEADS = 16
KEY_VALUE_HEADS = 8
HEAD_WIDTH = 128
EPSILON = 1e-06
MASKED = -1e30


def doc_positions(documents):
    indices = jnp.arange(documents.shape[-1], dtype=jnp.int32)
    boundary = jnp.concatenate(
        [
            jnp.ones(documents.shape[:-1] + (1,), dtype=jnp.bool_),
            documents[:, 1:] != documents[:, :-1],
        ],
        -1,
    )
    starts = lax.cummax(jnp.where(boundary, indices[None, :], 0), axis=1)
    return indices[None, :] - starts


def rope_tables(positions, head_size):
    middle = head_size // 2
    frequency = jnp.power(1000000.0, -2.0 * jnp.arange(middle, dtype=jnp.float32) / head_size)
    angles = positions.astype(jnp.float32)[:, None] * frequency[None, :]
    cosine_table = jnp.cos(angles)
    sine_table = jnp.sin(angles)
    return (
        jnp.concatenate([cosine_table, cosine_table], -1),
        jnp.concatenate([sine_table, sine_table], -1),
    )


def rotate(values):
    middle = values.shape[-1] // 2
    return jnp.concatenate([-values[..., middle:], values[..., :middle]], -1)


def rotate_back(values):
    middle = values.shape[-1] // 2
    return jnp.concatenate([values[..., middle:], -values[..., :middle]], -1)


def norm_parts(values):
    scaling = lax.rsqrt(jnp.mean(values * values, -1, keepdims=True) + EPSILON)
    return (values * scaling, scaling)


def norm_back(grad_normed, normed_hat, scaling, gains):
    scaled = grad_normed * gains
    return scaling * (scaled - normed_hat * jnp.mean(scaled * normed_hat, -1, keepdims=True))


def contract_rows(left, right):
    return lax.dot_general(
        left, right, (((0,), (0,)), ((), ())), preferred_element_type=jnp.float32
    )


def contract_cols(left, right):
    return lax.dot_general(
        left, right, (((1,), (1,)), ((), ())), preferred_element_type=jnp.float32
    )


def block_scores(query_rows, key_token_rows, doc_row, start, width, factor):
    scores = (
        jnp.einsum("qgrd,kgd->grqk", query_rows, key_token_rows, preferred_element_type=jnp.float32)
        * factor
    )
    query_index = start + jnp.arange(width)
    key_index = jnp.arange(key_token_rows.shape[0])
    allowed = (doc_row[start : start + width, None] == doc_row[None, :]) & (
        key_index[None, :] <= query_index[:, None]
    )
    return jnp.where(allowed, scores, MASKED)


def on_device(
    tokens,
    documents,
    cotangent,
    attn_gain,
    query_gain,
    key_norm_scale,
    query_weight,
    key_projection,
    value_projection,
    output_weight,
    mlp_gain,
    gate_weight,
    up_weight,
    down_weight,
):
    rows = tokens.shape[0]
    seqs, seq_length = documents.shape
    head_size = HEAD_WIDTH
    local_heads = QUERY_HEADS // lax.axis_size("mp")
    device_groups = KEY_VALUE_HEADS // lax.axis_size("mp")
    query_group = QUERY_HEADS // KEY_VALUE_HEADS
    block = min(512, seq_length)
    factor = head_size ** (-0.5)
    share = rows // lax.axis_size("mp")
    offset = lax.axis_index("mp") * share

    def take(values):
        return lax.dynamic_slice_in_dim(values, offset, share, 0)

    attn_parts = (
        lax.all_gather(attn_gain.astype(jnp.bfloat16), "dp", axis=0, tiled=True),
        lax.all_gather(query_gain.astype(jnp.bfloat16), "dp", axis=0, tiled=True),
        lax.all_gather(key_norm_scale.astype(jnp.bfloat16), "dp", axis=0, tiled=True),
        lax.all_gather(query_weight.astype(jnp.bfloat16), "dp", axis=0, tiled=True),
        lax.all_gather(key_projection.astype(jnp.bfloat16), "dp", axis=0, tiled=True),
        lax.all_gather(value_projection.astype(jnp.bfloat16), "dp", axis=0, tiled=True),
        lax.all_gather(output_weight.astype(jnp.bfloat16), "dp", axis=1, tiled=True),
    )
    gain_one = attn_parts[0].astype(jnp.float32)
    gain_query = attn_parts[1].astype(jnp.float32)
    gain_key = attn_parts[2].astype(jnp.float32)
    query_mat, key_mat, value_mat, output_mat = (
        attn_parts[3],
        attn_parts[4],
        attn_parts[5],
        attn_parts[6],
    )
    mlp_parts = (
        lax.all_gather(mlp_gain.astype(jnp.bfloat16), "dp", axis=0, tiled=True),
        lax.all_gather(gate_weight.astype(jnp.bfloat16), "dp", axis=0, tiled=True),
        lax.all_gather(up_weight.astype(jnp.bfloat16), "dp", axis=0, tiled=True),
        lax.all_gather(down_weight.astype(jnp.bfloat16), "dp", axis=1, tiled=True),
    )
    gain_two = mlp_parts[0].astype(jnp.float32)
    gate_mat, up_mat, down_mat = (mlp_parts[1], mlp_parts[2], mlp_parts[3])
    inputs = tokens.astype(jnp.float32)
    hat_one, inv_one = norm_parts(inputs)
    normed_one = (hat_one * gain_one).astype(jnp.bfloat16)
    query_raw = jnp.dot(normed_one, query_mat, preferred_element_type=jnp.float32)
    key_unnormed = jnp.dot(normed_one, key_mat, preferred_element_type=jnp.float32)
    value_token_rows = jnp.dot(normed_one, value_mat, preferred_element_type=jnp.float32).astype(
        jnp.bfloat16
    )
    positions = doc_positions(documents).reshape(rows)
    cosine_table, sine_table = rope_tables(positions, head_size)
    cosine_table = cosine_table[:, None, :]
    sine_table = sine_table[:, None, :]
    query_hat, query_inv = norm_parts(query_raw.reshape(rows, local_heads, head_size))
    key_hat, key_inv = norm_parts(key_unnormed.reshape(rows, device_groups, head_size))
    query_normed = query_hat * gain_query
    key_normed = key_hat * gain_key
    query_rows = (query_normed * cosine_table + rotate(query_normed) * sine_table).astype(
        jnp.bfloat16
    )
    key_token_rows = (key_normed * cosine_table + rotate(key_normed) * sine_table).astype(
        jnp.bfloat16
    )
    query_seq = query_rows.reshape(seqs, seq_length, device_groups, query_group, head_size)
    key_seq = key_token_rows.reshape(seqs, seq_length, device_groups, head_size)
    value_seq = value_token_rows.reshape(seqs, seq_length, device_groups, head_size)

    def attend_forward(items):
        seq_queries, seq_keys, seq_values, doc_row = items
        outputs = []
        log_totals = []
        for start in range(0, seq_length, block):
            scores = block_scores(
                seq_queries[start : start + block], seq_keys, doc_row, start, block, factor
            )
            highest = jnp.max(scores, -1, keepdims=True)
            exponent = jnp.exp(scores - highest)
            totals = jnp.sum(exponent, -1, keepdims=True)
            weights_block = (exponent / totals).astype(jnp.bfloat16)
            outputs.append(
                jnp.einsum(
                    "grqk,kgd->qgrd", weights_block, seq_values, preferred_element_type=jnp.float32
                )
            )
            log_totals.append(highest + jnp.log(totals))
        return (jnp.concatenate(outputs, 0), jnp.concatenate(log_totals, 2))

    attention_output, log_total = lax.map(
        attend_forward, (query_seq, key_seq, value_seq, documents)
    )
    attended_flat = attention_output.reshape(rows, local_heads * head_size).astype(jnp.bfloat16)
    attn_part = jnp.dot(attended_flat, output_mat, preferred_element_type=jnp.float32)
    hidden = inputs + lax.psum(attn_part, "mp")
    hat_two, inv_two = norm_parts(hidden)
    normed_two = (hat_two * gain_two).astype(jnp.bfloat16)
    hidden_share = take(hidden)
    gate_pre = jnp.dot(normed_two, gate_mat, preferred_element_type=jnp.float32)
    up_pre = jnp.dot(normed_two, up_mat, preferred_element_type=jnp.float32)
    sigmoid = jax.nn.sigmoid(gate_pre)
    swish = gate_pre * sigmoid
    active = (swish * up_pre).astype(jnp.bfloat16)
    mlp_part = jnp.dot(active, down_mat, preferred_element_type=jnp.float32)
    layer_output = (
        hidden_share + take(lax.psum(mlp_part.astype(jnp.bfloat16), "mp").astype(jnp.float32))
    ).astype(jnp.bfloat16)
    back_gain_one, back_gain_query, back_gain_key = (gain_one, gain_query, gain_key)
    back_query, back_key, back_value, back_output = (query_mat, key_mat, value_mat, output_mat)
    back_gate, back_up, back_down = (gate_mat, up_mat, down_mat)
    grad_out = cotangent.astype(jnp.float32)
    grad_active = contract_cols(cotangent, back_down)
    down_grad = contract_rows(active, cotangent)
    grad_gate = (grad_active * up_pre * sigmoid * (1.0 + gate_pre * (1.0 - sigmoid))).astype(
        jnp.bfloat16
    )
    grad_up = (grad_active * swish).astype(jnp.bfloat16)
    gate_grad = contract_rows(normed_two, grad_gate)
    up_grad = contract_rows(normed_two, grad_up)
    normed_two_part = contract_cols(grad_gate, back_gate) + contract_cols(grad_up, back_up)
    normed_two_grad = lax.psum(normed_two_part.astype(jnp.bfloat16), "mp").astype(jnp.float32)
    mlp_gain_part = jnp.sum(normed_two_grad * hat_two, 0)
    grad_hidden = grad_out + norm_back(normed_two_grad, hat_two, inv_two, gain_two)
    grad_hidden_low = grad_hidden.astype(jnp.bfloat16)
    grad_hidden_share = take(grad_hidden)
    output_grad = contract_rows(attended_flat, grad_hidden_low)
    grad_attended = contract_cols(grad_hidden_low, back_output).astype(jnp.bfloat16)
    grad_attended_seq = grad_attended.reshape(
        seqs, seq_length, device_groups, query_group, head_size
    )

    def attend_backward(items):
        seq_queries, seq_keys, seq_values, doc_row, seq_log_total, seq_grad = items
        query_grads = []
        key_grad = jnp.zeros((seq_length, device_groups, head_size), jnp.float32)
        value_grad = jnp.zeros((seq_length, device_groups, head_size), jnp.float32)
        for start in range(0, seq_length, block):
            block_queries = seq_queries[start : start + block]
            block_grad = seq_grad[start : start + block]
            scores = block_scores(block_queries, seq_keys, doc_row, start, block, factor)
            weights_block = jnp.exp(scores - seq_log_total[:, :, start : start + block])
            grad_weights = jnp.einsum(
                "qgrd,kgd->grqk", block_grad, seq_values, preferred_element_type=jnp.float32
            )
            inner = jnp.sum(weights_block * grad_weights, -1, keepdims=True)
            grad_scores = (weights_block * (grad_weights - inner)).astype(jnp.bfloat16)
            query_grads.append(
                jnp.einsum(
                    "grqk,kgd->qgrd", grad_scores, seq_keys, preferred_element_type=jnp.float32
                )
                * factor
            )
            key_grad = (
                key_grad
                + jnp.einsum(
                    "grqk,qgrd->kgd", grad_scores, block_queries, preferred_element_type=jnp.float32
                )
                * factor
            )
            value_grad = value_grad + jnp.einsum(
                "grqk,qgrd->kgd",
                weights_block.astype(jnp.bfloat16),
                block_grad,
                preferred_element_type=jnp.float32,
            )
        return (jnp.concatenate(query_grads, 0), key_grad, value_grad)

    query_rot_grad, key_rot_grad, value_seq_grad = lax.map(
        attend_backward, (query_seq, key_seq, value_seq, documents, log_total, grad_attended_seq)
    )
    query_rot_grad = query_rot_grad.reshape(rows, local_heads, head_size)
    key_rot_grad = key_rot_grad.reshape(rows, device_groups, head_size)
    query_norm_grad = query_rot_grad * cosine_table + rotate_back(query_rot_grad * sine_table)
    key_norm_grad = key_rot_grad * cosine_table + rotate_back(key_rot_grad * sine_table)
    query_gain_part = jnp.sum(query_norm_grad * query_hat, (0, 1))
    key_gain_part = jnp.sum(key_norm_grad * key_hat, (0, 1))
    query_raw_grad = (
        norm_back(query_norm_grad, query_hat, query_inv, back_gain_query)
        .reshape(rows, local_heads * head_size)
        .astype(jnp.bfloat16)
    )
    key_raw_grad = (
        norm_back(key_norm_grad, key_hat, key_inv, back_gain_key)
        .reshape(rows, device_groups * head_size)
        .astype(jnp.bfloat16)
    )
    value_raw_grad = value_seq_grad.reshape(rows, device_groups * head_size).astype(jnp.bfloat16)
    query_grad = contract_rows(normed_one, query_raw_grad)
    key_grad = contract_rows(normed_one, key_raw_grad)
    value_grad = contract_rows(normed_one, value_raw_grad)
    normed_one_part = (
        contract_cols(query_raw_grad, back_query)
        + contract_cols(key_raw_grad, back_key)
        + contract_cols(value_raw_grad, back_value)
    )
    hat_one_share = take(hat_one)
    inv_one_share = take(inv_one)
    normed_one_grad, query_gain_sum, key_gain_sum = (
        lax.psum(normed_one_part.astype(jnp.bfloat16), "mp").astype(jnp.float32),
        lax.psum(query_gain_part.astype(jnp.bfloat16), "mp").astype(jnp.float32),
        lax.psum(key_gain_part.astype(jnp.bfloat16), "mp").astype(jnp.float32),
    )
    attn_gain_total = jnp.sum(normed_one_grad * hat_one, 0)
    input_grad = grad_hidden_share + norm_back(
        take(normed_one_grad), hat_one_share, inv_one_share, back_gain_one
    )
    attn_grads = (
        lax.psum_scatter(
            attn_gain_total.astype(jnp.bfloat16), "dp", scatter_dimension=0, tiled=True
        ).astype(jnp.float32),
        lax.psum_scatter(
            query_gain_sum.astype(jnp.bfloat16), "dp", scatter_dimension=0, tiled=True
        ).astype(jnp.float32),
        lax.psum_scatter(
            key_gain_sum.astype(jnp.bfloat16), "dp", scatter_dimension=0, tiled=True
        ).astype(jnp.float32),
        lax.psum_scatter(
            query_grad.astype(jnp.bfloat16), "dp", scatter_dimension=0, tiled=True
        ).astype(jnp.float32),
        lax.psum_scatter(
            key_grad.astype(jnp.bfloat16), "dp", scatter_dimension=0, tiled=True
        ).astype(jnp.float32),
        lax.psum_scatter(
            value_grad.astype(jnp.bfloat16), "dp", scatter_dimension=0, tiled=True
        ).astype(jnp.float32),
        lax.psum_scatter(
            output_grad.astype(jnp.bfloat16), "dp", scatter_dimension=1, tiled=True
        ).astype(jnp.float32),
    )
    mlp_grads = (
        lax.psum_scatter(
            mlp_gain_part.astype(jnp.bfloat16), "dp", scatter_dimension=0, tiled=True
        ).astype(jnp.float32),
        lax.psum_scatter(
            gate_grad.astype(jnp.bfloat16), "dp", scatter_dimension=0, tiled=True
        ).astype(jnp.float32),
        lax.psum_scatter(
            up_grad.astype(jnp.bfloat16), "dp", scatter_dimension=0, tiled=True
        ).astype(jnp.float32),
        lax.psum_scatter(
            down_grad.astype(jnp.bfloat16), "dp", scatter_dimension=1, tiled=True
        ).astype(jnp.float32),
    )
    return (
        layer_output,
        input_grad,
        attn_grads[0],
        attn_grads[1],
        attn_grads[2],
        attn_grads[3],
        attn_grads[4],
        attn_grads[5],
        attn_grads[6],
        mlp_grads[0],
        mlp_grads[1],
        mlp_grads[2],
        mlp_grads[3],
    )


def solution(mesh):
    in_specs = (
        P("dp", None),
        P("dp", None),
        P("dp", None),
        P("dp"),
        P("dp"),
        P("dp"),
        P("dp", "mp"),
        P("dp", "mp"),
        P("dp", "mp"),
        P("mp", "dp"),
        P("dp"),
        P("dp", "mp"),
        P("dp", "mp"),
        P("mp", "dp"),
    )
    out_specs = (
        P(("dp", "mp"), None),
        P(("dp", "mp"), None),
        P("dp"),
        P("dp"),
        P("dp"),
        P("dp", "mp"),
        P("dp", "mp"),
        P("dp", "mp"),
        P("mp", "dp"),
        P("dp"),
        P("dp", "mp"),
        P("dp", "mp"),
        P("mp", "dp"),
    )
    return jax.shard_map(
        on_device, mesh=mesh, in_specs=in_specs, out_specs=out_specs, check_vma=False
    )
```

profile of v0, /device:TPU:0, one launch (start us, length us, event | category | flops | bytes accessed | tf_op | source)
XLA Modules:
  0.0 1635.1 jit_solution(17745862805396485269)
XLA Ops:
  16.6 22.3 %all-gather = bf16[8,1,256]{2,1,0:T(2,128)(2,1)S(1)} all-gather(bf16[1,1,256]{2,1,0:T(2,128)(2,1)S(1)} %reshape.304), channel_id=1, replica_groups=mesh['dp'=8,'mp'=4] {'dp'}, dimensions={0}, use_global_device_ids=true | all-gather | bytes 4608 | tf_op jit(solution)/shard_map/all_gather | solution.py:114
  43.8 17.2 %all-reduce.7 = (bf16[128]{0:T(256)(128)(2,1)S(1)}, bf16[128]{0:T(256)(128)(2,1)S(1)}) all-reduce(bf16[128]{0:T(256)(128)(2,1)S(1)} %dynamic-update-slice, bf16[128]{0:T(256)(128)(2,1)S(1)} %dynamic-update-slice.1), channel_id=1, replica_groups=mesh['dp'=8,'mp'=4] {'dp'}, use_global_device_ids=true, to_apply=%add | all-reduce | flops 256 | bytes 1024
  63.7 4.0 multiply_reduce_fusion.7
  69.1 26.4 %all-gather.10.cloned.1.call-done = bf16[2048,256]{1,0:T(8,128)(2,1)} async-done(((bf16[256,256]{1,0:T(8,128)(2,1)}), bf16[2048,256]{1,0:T(8,128)(2,1)}) %all-gather.10.cloned.1.call-update) | async-done | bytes 1048592 | tf_op jit(solution)/shard_map/all_gather | solution.py:119
  95.5 4.0 convolution_convert_fusion.8
  99.5 46.8 %all-gather.14.cloned.1.call-done = bf16[2048,512]{1,0:T(8,128)(2,1)} async-done(((bf16[256,512]{1,0:T(8,128)(2,1)}), bf16[2048,512]{1,0:T(8,128)(2,1)}) %all-gather.14.cloned.1.call-update) | async-done | bytes 2097168 | tf_op jit(solution)/shard_map/all_gather | solution.py:117
  146.3 5.4 multiply_reduce_fusion.4
  164.0 34.4 %all-gather.16.cloned.1.call-done = bf16[512,2048]{1,0:T(8,128)(2,1)} async-done(((bf16[512,256]{1,0:T(8,128)(2,1)}), bf16[512,2048]{1,0:T(8,128)(2,1)}) %all-gather.16.cloned.1.call-update) | async-done | bytes 2097168 | tf_op jit(solution)/shard_map/all_gather | solution.py:120
  198.4 7.2 fusion.77
  212.0 17.4 %all-gather.1 = bf16[8,1,256]{2,1,0:T(2,128)(2,1)S(1)} all-gather(bf16[1,1,256]{2,1,0:T(2,128)(2,1)S(1)} %reshape.306), channel_id=1, replica_groups=mesh['dp'=8,'mp'=4] {'dp'}, dimensions={0}, use_global_device_ids=true | all-gather | bytes 4608 | tf_op jit(solution)/shard_map/all_gather | solution.py:132
  230.0 126.9 %all-reduce.14.cloned.1.call-done = f32[1024,2048]{1,0:T(8,128)} async-done(((f32[1024,2048]{1,0:T(8,128)}), f32[1024,2048]{1,0:T(8,128)}) %all-reduce.14.cloned.1.call-update) | async-done | bytes 8388624 | tf_op jit(solution)/shard_map/psum | solution.py:190
  356.8 5.7 multiply_reduce_fusion.1
  362.6 3.3 copy-done.2
  368.6 90.1 %all-gather.18.cloned.1.call-done = bf16[2048,1536]{1,0:T(8,128)(2,1)} async-done(((bf16[256,1536]{1,0:T(8,128)(2,1)}), bf16[2048,1536]{1,0:T(8,128)(2,1)}) %all-gather.18.cloned.1.call-update) | async-done | bytes 6291472 | tf_op jit(solution)/shard_map/all_gather | solution.py:133
  458.7 11.9 fusion.78
  470.6 88.1 %all-gather.20.cloned.1.call-done = bf16[2048,1536]{1,0:T(8,128)(2,1)} async-done(((bf16[256,1536]{1,0:T(8,128)(2,1)}), bf16[2048,1536]{1,0:T(8,128)(2,1)}) %all-gather.20.cloned.1.call-update) | async-done | bytes 6291472 | tf_op jit(solution)/shard_map/all_gather | solution.py:134
  558.7 11.7 fusion.79
  570.4 89.1 %all-gather.22.cloned.1.call-done = bf16[1536,2048]{1,0:T(8,128)(2,1)} async-done(((bf16[1536,256]{1,0:T(8,128)(2,1)}), bf16[1536,2048]{1,0:T(8,128)(2,1)}) %all-gather.22.cloned.1.call-update) | async-done | bytes 6291472 | tf_op jit(solution)/shard_map/all_gather | solution.py:135
  659.4 16.4 %multiply_convert_fusion.2 = (bf16[1024,1536]{1,0:T(8,128)(2,1)}, bf16[1024,1536]{1,0:T(8,128)(2,1)S(1)}, bf16[1024,1536]{1,0:T(8,128)(2,1)}) fusion(f32[1024,1536]{1,0:T(8,128)} %fusion.78, f32[1024,1536]{1,0:T(8,128)} %fusion.79, bf16[1024,2048]{1,0:T(8,128)(2,1)} %param.16, bf16[1536,2048]{1,0:T(8,128)(2,1)} %all-gather.22.cloned.1.call-done), kind=kOutput, calls=%fused_computation.43 | convolution fusion | flops 6466043904 | bytes 32505856 | tf_op jit(solution)/shard_map/dot_general | solution.py:65
  675.8 10.0 fusion.80
  685.8 10.2 add_convert_fusion.1
  696.2 11.3 convolution_convert_fusion.3
  707.5 72.4 %all-reduce.16.cloned.1.call-done = bf16[1024,2048]{1,0:T(8,128)(2,1)} async-done(((bf16[1024,2048]{1,0:T(8,128)(2,1)}), bf16[1024,2048]{1,0:T(8,128)(2,1)}) %all-reduce.16.cloned.1.call-update) | async-done | bytes 4194320 | tf_op jit(solution)/shard_map/psum | solution.py:216
  779.9 6.0 fusion.5
  787.0 5.0 fusion.4
  800.2 5.0 fusion.7
  805.2 5.1 fusion.9
  828.8 4.9 convolution_convert_fusion.6
  833.9 5.1 fusion.33
  843.4 3.3 add_convert_fusion
  846.8 4.9 convolution_convert_fusion.7
  851.8 6.5 convolution_convert_fusion.5
  858.6 7.1 convolution_convert_fusion.4
  865.8 11.5 convolution_convert_fusion.2
  879.2 11.0 convolution_convert_fusion.1
  892.1 10.9 convolution_convert_fusion
  906.1 146.2 %all-reduce.18.cloned.1.call-done = (bf16[1024,2048]{1,0:T(8,128)(2,1)}, bf16[1024,2048]{1,0:T(8,128)(2,1)}) async-done(((bf16[1024,2048]{1,0:T(8,128)(2,1)}, bf16[1024,2048]{1,0:T(8,128)(2,1)}), (bf16[1024,2048]{1,0:T(8,128)(2,1)}, bf16[1024,2048]{1,0:T(8,128)(2,1)})) %all-reduce.18.cloned.1.call-update) | async-done | bytes 8388624 | tf_op jit(solution)/shard_map/psum | solution.py:201
  1052.2 6.5 multiply_reduce_fusion
  1058.8 22.0 %all-reduce.6 = (bf16[2048]{0:T(1024)(128)(2,1)S(1)}, bf16[128]{0:T(256)(128)(2,1)S(1)}, bf16[128]{0:T(256)(128)(2,1)S(1)}, bf16[2048]{0:T(1024)(128)(2,1)S(1)}) all-reduce(bf16[2048]{0:T(1024)(128)(2,1)S(1)} %get-tuple-element.84, bf16[128]{0:T(256)(128)(2,1)S(1)} %reduce_sum.170, ...), channel_id=2, replica_groups=mesh['dp'=8,'mp'=4] {'dp'}, use_global_device_ids=true, to_apply=%region_21.22.clone | all-reduce | flops 4352 | bytes 17408
  1081.0 38.8 %reduce-scatter.10.cloned.1.call-done = bf16[256,256]{1,0:T(8,128)(2,1)} async-done(((bf16[2048,256]{1,0:T(8,128)(2,1)}), bf16[256,256]{1,0:T(8,128)(2,1)}) %reduce-scatter.10.cloned.1.call-update) | async-done | bytes 131088 | tf_op jit(solution)/shard_map/reduce_scatter | solution.py:315
  1121.4 5.6 all-reduce.8
  1127.0 6.7 convert_element_type.272
  1134.7 56.6 %reduce-scatter.8.cloned.1.call-done = bf16[256,512]{1,0:T(8,128)(2,1)} async-done(((bf16[2048,512]{1,0:T(8,128)(2,1)}), bf16[256,512]{1,0:T(8,128)(2,1)}) %reduce-scatter.8.cloned.1.call-update) | async-done | bytes 262160 | tf_op jit(solution)/shard_map/reduce_scatter | solution.py:312
  1193.1 69.3 %reduce-scatter.14.cloned.1.call-done = bf16[512,256]{1,0:T(8,128)(2,1)} async-done(((bf16[512,2048]{1,0:T(8,128)(2,1)}), bf16[512,256]{1,0:T(8,128)(2,1)}) %reduce-scatter.14.cloned.1.call-update) | async-done | bytes 262160 | tf_op jit(solution)/shard_map/reduce_scatter | solution.py:321
  1267.3 6.0 multiply_add_fusion
  1273.3 110.0 %reduce-scatter.16.cloned.1.call-done = bf16[256,1536]{1,0:T(8,128)(2,1)} async-done(((bf16[2048,1536]{1,0:T(8,128)(2,1)}), bf16[256,1536]{1,0:T(8,128)(2,1)}) %reduce-scatter.16.cloned.1.call-update) | async-done | bytes 786448 | tf_op jit(solution)/shard_map/reduce_scatter | solution.py:329
  1385.7 118.5 %reduce-scatter.18.cloned.1.call-done = bf16[256,1536]{1,0:T(8,128)(2,1)} async-done(((bf16[2048,1536]{1,0:T(8,128)(2,1)}), bf16[256,1536]{1,0:T(8,128)(2,1)}) %reduce-scatter.18.cloned.1.call-update) | async-done | bytes 786448 | tf_op jit(solution)/shard_map/reduce_scatter | solution.py:332
  1506.7 119.0 %reduce-scatter.20.cloned.1.call-done = bf16[1536,256]{1,0:T(8,128)(2,1)} async-done(((bf16[1536,2048]{1,0:T(8,128)(2,1)}), bf16[1536,256]{1,0:T(8,128)(2,1)}) %reduce-scatter.20.cloned.1.call-update) | async-done | bytes 786448 | tf_op jit(solution)/shard_map/reduce_scatter | solution.py:335
  (257 shorter events, 94.1 us)
Async XLA Ops:
  7.2 34.9 %copy-start.45 = (u32[32]{0:T(128)S(1)}, u32[32]{0:T(128)}, u32[]{:S(2)}) copy-start(u32[32]{0:T(128)} %constant.106) | copy-start | bytes 388
  7.2 34.8 %copy-start.50 = (f32[16]{0:T(128)S(1)}, f32[16]{0:T(128)}, u32[]{:S(2)}) copy-start(f32[16]{0:T(128)} %param.19) | copy-start | bytes 196
  7.2 34.8 %copy-start.51 = (f32[16]{0:T(128)S(1)}, f32[16]{0:T(128)}, u32[]{:S(2)}) copy-start(f32[16]{0:T(128)} %param.18) | copy-start | bytes 196
  7.2 56.4 %all-gather.12.cloned.1.call-start = ((), (), s32[]{:S(2)}) async-start(), calls=%async_computation.8 | async-start | bytes 1179648 | tf_op jit(solution)/shard_map/all_gather | solution.py:118
  8.9 86.6 %all-gather.10.cloned.1.call-start = ((), (), s32[]{:S(2)}) async-start(), calls=%async_computation.7 | async-start | bytes 1179648 | tf_op jit(solution)/shard_map/all_gather | solution.py:119
  10.6 52.3 %copy-start.39 = (s32[1,1024]{1,0:T(1,128)S(1)}, s32[1,1024]{1,0:T(1,128)}, u32[]{:S(2)}) copy-start(s32[1,1024]{1,0:T(1,128)} %param.15) | copy-start | bytes 12292
  10.6 135.7 %all-gather.14.cloned.1.call-start = ((), (), s32[]{:S(2)}) async-start(), calls=%async_computation.9 | async-start | bytes 2359296 | tf_op jit(solution)/shard_map/all_gather | solution.py:117
  12.5 185.9 %all-gather.16.cloned.1.call-start = ((), (), s32[]{:S(2)}) async-start(), calls=%async_computation.10 | async-start | bytes 2359296 | tf_op jit(solution)/shard_map/all_gather | solution.py:120
  14.3 342.5 %all-reduce.14.cloned.1.call-start = ((), (), s32[]{:S(2)}) async-start(), calls=%async_computation.11 | async-start | bytes 16777216 | tf_op jit(solution)/shard_map/psum | solution.py:190
  38.9 107.4 %copy-start.37 = (f32[8,1,256]{2,1,0:T(1,128)}, f32[8,1,256]{2,1,0:T(1,128)S(1)}, u32[]{:S(2)}) copy-start(f32[8,1,256]{2,1,0:T(1,128)S(1)} %convert_element_type.295) | copy-start | bytes 24580
  42.0 104.3 %copy-start.40 = (f32[1024]{0:T(1024)}, f32[1024]{0:T(1024)S(1)}, u32[]{:S(2)}) copy-start(f32[1024]{0:T(1024)S(1)} %add_rsqrt_fusion.3) | copy-start | bytes 12292
  61.0 7.0 copy-start.43
  62.9 89.5 %copy-start.7 = (f32[1024,128]{0,1:T(8,128)}, f32[1024,128]{0,1:T(8,128)S(1)}, u32[]{:S(2)}) copy-start(f32[1024,128]{0,1:T(8,128)S(1)} %pad_maximum_fusion.4) | copy-start | bytes 1572868
  62.9 89.4 %copy-start.9 = (f32[1024,128]{0,1:T(8,128)}, f32[1024,128]{0,1:T(8,128)S(1)}, u32[]{:S(2)}) copy-start(f32[1024,128]{0,1:T(8,128)S(1)} %pad_maximum_fusion.5) | copy-start | bytes 1572868
  69.1 88.1 %copy-start.16 = (bf16[1024,2,128,1]{0,2,3,1:T(8,128)(2,1)}, bf16[1024,2,128,1]{0,2,3,1:T(8,128)(2,1)S(1)}, u32[]{:S(2)}) copy-start(bf16[1024,2,128,1]{0,2,3,1:T(8,128)(2,1)S(1)} %fusion.64) | copy-start | bytes 1572868
  153.9 3.3 copy-start.20
  155.6 4.5 copy-start
  163.9 41.7 %copy-start.33 = (bf16[1024,2,2,128]{0,3,2,1:T(8,128)(2,1)}, bf16[1024,2,2,128]{0,3,2,1:T(8,128)(2,1)S(1)}, u32[]{:S(2)}) copy-start(bf16[1024,2,2,128]{0,3,2,1:T(8,128)(2,1)S(1)} %pad_maximum_fusion.3) | copy-start | bytes 3145732
  205.6 6.3 copy-start.49
  205.6 253.0 %all-gather.18.cloned.1.call-start = ((), (), s32[]{:S(2)}) async-start(), calls=%async_computation.12 | async-start | bytes 7077888 | tf_op jit(solution)/shard_map/all_gather | solution.py:133
  208.0 350.7 %all-gather.20.cloned.1.call-start = ((), (), s32[]{:S(2)}) async-start(), calls=%async_computation.13 | async-start | bytes 7077888 | tf_op jit(solution)/shard_map/all_gather | solution.py:134
  210.8 448.6 %all-gather.22.cloned.1.call-start = ((), (), s32[]{:S(2)}) async-start(), calls=%async_computation.14 | async-start | bytes 7077888 | tf_op jit(solution)/shard_map/all_gather | solution.py:135
  211.9 568.0 %all-reduce.16.cloned.1.call-start = ((), (), s32[]{:S(2)}) async-start(), calls=%async_computation.15 | async-start | bytes 8388608 | tf_op jit(solution)/shard_map/psum | solution.py:216
  675.8 10.0 copy-start.52
  675.8 10.0 copy-start.46
  696.1 208.3 %reduce-scatter.12.cloned.1.call-start = ((), (), s32[]{:S(2)}) async-start(), calls=%async_computation.18 | async-start | bytes 1179648 | tf_op jit(solution)/shard_map/reduce_scatter | solution.py:318
  779.9 6.0 copy-start.12
  779.9 7.1 copy-start.24
  779.9 15.5 slice-start
  787.0 5.0 copy-start.48
  787.0 8.5 slice-start.1
  792.0 3.3 copy-start.15
  795.5 4.4 slice-start.2
  805.2 5.1 copy-start.21
  814.0 12.5 copy-start.13
  820.4 6.2 copy-start.14
  828.7 5.2 copy-start.42
  833.7 218.6 %all-reduce.18.cloned.1.call-start = ((), (), s32[]{:S(2)}) async-start(), calls=%async_computation.23 | async-start | bytes 16777216 | tf_op jit(solution)/shard_map/psum | solution.py:201
  833.9 5.1 copy-start.22
  833.9 5.4 copy-start.29
  846.7 5.0 copy-start.32
  846.7 273.0 %reduce-scatter.10.cloned.1.call-start = ((), (), s32[]{:S(2)}) async-start(), calls=%async_computation.17 | async-start | bytes 1179648 | tf_op jit(solution)/shard_map/reduce_scatter | solution.py:315
  851.7 6.9 copy-start.34
  851.7 339.5 %reduce-scatter.8.cloned.1.call-start = ((), (), s32[]{:S(2)}) async-start(), calls=%async_computation.16 | async-start | bytes 2359296 | tf_op jit(solution)/shard_map/reduce_scatter | solution.py:312
  858.3 404.0 %reduce-scatter.14.cloned.1.call-start = ((), (), s32[]{:S(2)}) async-start(), calls=%async_computation.19 | async-start | bytes 2359296 | tf_op jit(solution)/shard_map/reduce_scatter | solution.py:321
  865.7 517.5 %reduce-scatter.16.cloned.1.call-start = ((), (), s32[]{:S(2)}) async-start(), calls=%async_computation.20 | async-start | bytes 7077888 | tf_op jit(solution)/shard_map/reduce_scatter | solution.py:329
  877.3 627.0 %reduce-scatter.18.cloned.1.call-start = ((), (), s32[]{:S(2)}) async-start(), calls=%async_computation.21 | async-start | bytes 7077888 | tf_op jit(solution)/shard_map/reduce_scatter | solution.py:332
  890.2 735.5 %reduce-scatter.20.cloned.1.call-start = ((), (), s32[]{:S(2)}) async-start(), calls=%async_computation.22 | async-start | bytes 7077888 | tf_op jit(solution)/shard_map/reduce_scatter | solution.py:335
  (28 other events, 52.7 us)
Sparse Core Ops, SparseCore 0:
  10.7 42.9 all-gather.11
  56.4 39.0 all-gather.9
  98.2 48.0 all-gather.13
  148.8 49.5 all-gather.15
  205.8 151.0 all-reduce.13
  359.5 99.1 all-gather.17
  461.4 97.1 all-gather.19
  561.3 98.1 all-gather.21
  696.2 83.6 all-reduce.15
  833.8 63.5 reduce-scatter.11
  900.0 152.2 all-reduce.17
  1056.1 63.6 reduce-scatter.9
  1124.3 66.9 reduce-scatter.7
  1195.0 67.2 reduce-scatter.13
  1266.2 117.0 reduce-scatter.15
  1387.1 117.0 reduce-scatter.17
  1508.2 117.5 reduce-scatter.19
where the time goes:
time: 1650 us; the launch traced here: 1640 us
  waiting for transfers between devices  1230 us (75%)
  matrix products  182 us (11%)
  other arithmetic  98.9 us (6%)
  blocking collectives  84.5 us (5%)
  local copies, waits for them, and re-layouts  17.7 us (1%)
  between operations  17.4 us (1%)
    psum x1, waiting for transfers between devices, on_device(): lax.psum(mlp_part.astype(jnp.bfloat16), 'mp').astype(jnp.float32)  146 us
    psum x1, waiting for transfers between devices, on_device(): hidden = inputs + lax.psum(attn_part, 'mp')  127 us
    reduce_scatter x1, waiting for transfers between devices, on_device(): lax.psum_scatter(down_grad.astype(jnp.bfloat16), 'dp', scatter_dimension=...  119 us
    reduce_scatter x1, waiting for transfers between devices, on_device(): lax.psum_scatter(up_grad.astype(jnp.bfloat16), 'dp', scatter_dimension=0,...  119 us
    reduce_scatter x1, waiting for transfers between devices, on_device(): lax.psum_scatter(gate_grad.astype(jnp.bfloat16), 'dp', scatter_dimension=...  110 us
    all_gather x1, waiting for transfers between devices, on_device(): lax.all_gather(gate_weight.astype(jnp.bfloat16), 'dp', axis=0, tiled=True)  90.1 us
    all_gather x1, waiting for transfers between devices, on_device(): lax.all_gather(down_weight.astype(jnp.bfloat16), 'dp', axis=1, tiled=True)  89.1 us
    all_gather x1, waiting for transfers between devices, on_device(): lax.all_gather(up_weight.astype(jnp.bfloat16), 'dp', axis=0, tiled=True)  88.1 us
  transfers between devices with their start and end apart: 17, of which 15 were waited for; matrix products, arithmetic and copies ran while one was open for 11% of the time, Pallas kernels for 0%

commit v1 on v0

--- a/solution.py
+++ b/solution.py
@@ -8,6 +8,19 @@
 HEAD_WIDTH = 128
 EPSILON = 1e-06
 MASKED = -1e30
+
+
+def collect(shard, axis, dim):
+    ways = lax.axis_size(axis)
+    up = [(d, (d + 1) % ways) for d in range(ways)]
+    down = [(d, (d - 1) % ways) for d in range(ways)]
+    earlier, later = ([shard], [shard])
+    for _ in range(ways // 2):
+        earlier.append(lax.ppermute(earlier[-1], axis, up))
+    for _ in range((ways - 1) // 2):
+        later.append(lax.ppermute(later[-1], axis, down))
+    line = jnp.concatenate([*earlier[::-1], *later[1:]], axis=dim)
+    return jnp.roll(line, (lax.axis_index(axis) - ways // 2) * shard.shape[dim], axis=dim)
 
 
 def doc_positions(documents):
@@ -132,7 +145,7 @@
         lax.all_gather(mlp_gain.astype(jnp.bfloat16), "dp", axis=0, tiled=True),
         lax.all_gather(gate_weight.astype(jnp.bfloat16), "dp", axis=0, tiled=True),
         lax.all_gather(up_weight.astype(jnp.bfloat16), "dp", axis=0, tiled=True),
-        lax.all_gather(down_weight.astype(jnp.bfloat16), "dp", axis=1, tiled=True),
+        collect(down_weight.astype(jnp.bfloat16), "dp", 1),
     )
     gain_two = mlp_parts[0].astype(jnp.float32)
     gate_mat, up_mat, down_mat = (mlp_parts[1], mlp_parts[2], mlp_parts[3])

time: 1650 us -> 1550 us (0.939)
  waiting for transfers between devices: 1230 us -> 1070 us
  starting transfers between devices: 1.34 us -> 30.2 us
  local copies, waits for them, and re-layouts: 17.7 us -> 42.3 us
    psum x1, waiting for transfers between devices: 127 us -> 0.01 us  [on_device(): hidden = inputs + lax.psum(attn_part, 'mp')]
    all_gather x1 -> x0, waiting for transfers between devices: 89.1 us -> none  [on_device(): lax.all_gather(down_weight.astype(jnp.bfloat16), 'dp', axis=1, tiled=True)]
    ppermute x0 -> x7, waiting for transfers between devices: none -> 64.7 us  [the longest x4 59.7 us: collect(): earlier.append(lax.ppermute(earlier[-1], axis, up))]
    reduce_scatter x1, waiting for transfers between devices: 0.01 us -> 38.9 us  [on_device(): lax.psum_scatter(value_grad.astype(jnp.bfloat16), 'dp', scatter_dimension...]
    reduce_scatter x1, waiting for transfers between devices: 38.8 us -> 0.02 us  [on_device(): lax.psum_scatter(key_grad.astype(jnp.bfloat16), 'dp', scatter_dimension=0...]
    ppermute x0 -> x7, starting transfers between devices: none -> 28.9 us  [the longest x3 22.3 us: collect(): later.append(lax.ppermute(later[-1], axis, down))]
    unnamed x127 -> x176, local copies, waits for them, and re-layouts: 15.9 us -> 40.1 us
  transfers between devices with their start and end apart: 17 -> 23, of which waited for: 15 -> 17; matrix products, arithmetic and copies ran while one was open for 11% -> 13% of each run, Pallas kernels for 0% -> 0%
where the time goes in v1:
time: 1550 us; the launch traced here: 1540 us
  waiting for transfers between devices  1070 us (69%)
  matrix products  182 us (12%)
  blocking collectives  98.4 us (6%)
  other arithmetic  96.3 us (6%)
  local copies, waits for them, and re-layouts  42.3 us (3%)
  starting transfers between devices  30.2 us (2%)
  between operations  17.6 us (1%)
    psum x1, waiting for transfers between devices, on_device(): lax.psum(mlp_part.astype(jnp.bfloat16), 'mp').astype(jnp.float32)  137 us
    reduce_scatter x1, waiting for transfers between devices, on_device(): lax.psum_scatter(down_grad.astype(jnp.bfloat16), 'dp', scatter_dimension=...  119 us
    reduce_scatter x1, waiting for transfers between devices, on_device(): lax.psum_scatter(up_grad.astype(jnp.bfloat16), 'dp', scatter_dimension=0,...  119 us
    reduce_scatter x1, waiting for transfers between devices, on_device(): lax.psum_scatter(gate_grad.astype(jnp.bfloat16), 'dp', scatter_dimension=...  110 us
    all_gather x1, waiting for transfers between devices, on_device(): lax.all_gather(up_weight.astype(jnp.bfloat16), 'dp', axis=0, tiled=True)  88.1 us
    all_gather x1, waiting for transfers between devices, on_device(): lax.all_gather(gate_weight.astype(jnp.bfloat16), 'dp', axis=0, tiled=True)  87.3 us
    psum x1, waiting for transfers between devices, on_device(): lax.psum(normed_two_part.astype(jnp.bfloat16), 'mp').astype(jnp.float32)  72.6 us
    reduce_scatter x1, waiting for transfers between devices, on_device(): lax.psum_scatter(output_grad.astype(jnp.bfloat16), 'dp', scatter_dimensio...  69.5 us
  transfers between devices with their start and end apart: 23, of which 17 were waited for; matrix products, arithmetic and copies ran while one was open for 13% of the time, Pallas kernels for 0%

profile of v1, /device:TPU:0, one launch (start us, length us, event | category | flops | bytes accessed | tf_op | source)
XLA Modules:
  0.0 1538.2 jit_solution(12975955192849788757)
XLA Ops:
  16.6 22.3 %all-gather = bf16[8,1,256]{2,1,0:T(2,128)(2,1)S(1)} all-gather(bf16[1,1,256]{2,1,0:T(2,128)(2,1)S(1)} %reshape.304), channel_id=1, replica_groups=mesh['dp'=8,'mp'=4] {'dp'}, dimensions={0}, use_global_device_ids=true | all-gather | bytes 4608 | tf_op jit(solution)/shard_map/all_gather | solution.py:127
  43.8 17.2 %all-reduce.7 = (bf16[128]{0:T(256)(128)(2,1)S(1)}, bf16[128]{0:T(256)(128)(2,1)S(1)}) all-reduce(bf16[128]{0:T(256)(128)(2,1)S(1)} %dynamic-update-slice, bf16[128]{0:T(256)(128)(2,1)S(1)} %dynamic-update-slice.1), channel_id=1, replica_groups=mesh['dp'=8,'mp'=4] {'dp'}, use_global_device_ids=true, to_apply=%add | all-reduce | flops 256 | bytes 1024
  63.7 4.0 multiply_reduce_fusion.7
  69.1 26.5 %all-gather.9.cloned.1.call-done = bf16[2048,256]{1,0:T(8,128)(2,1)} async-done(((bf16[256,256]{1,0:T(8,128)(2,1)}), bf16[2048,256]{1,0:T(8,128)(2,1)}) %all-gather.9.cloned.1.call-update) | async-done | bytes 1048592 | tf_op jit(solution)/shard_map/all_gather | solution.py:132
  99.6 46.8 %all-gather.13.cloned.1.call-done = bf16[2048,512]{1,0:T(8,128)(2,1)} async-done(((bf16[256,512]{1,0:T(8,128)(2,1)}), bf16[2048,512]{1,0:T(8,128)(2,1)}) %all-gather.13.cloned.1.call-update) | async-done | bytes 2097168 | tf_op jit(solution)/shard_map/all_gather | solution.py:130
  146.4 5.4 multiply_reduce_fusion.4
  163.5 35.0 %all-gather.15.cloned.1.call-done = bf16[512,2048]{1,0:T(8,128)(2,1)} async-done(((bf16[512,256]{1,0:T(8,128)(2,1)}), bf16[512,2048]{1,0:T(8,128)(2,1)}) %all-gather.15.cloned.1.call-update) | async-done | bytes 2097168 | tf_op jit(solution)/shard_map/all_gather | solution.py:133
  198.5 7.3 fusion.90
  212.3 17.4 %collective-permute-done = bf16[1536,256]{1,0:T(8,128)(2,1)S(1)} collective-permute-done((bf16[1536,256]{1,0:T(8,128)(2,1)S(1)}, bf16[1536,256]{1,0:T(8,128)(2,1)S(1)}, u32[]{:S(2)}, u32[]{:S(2)}) %collective-permute-start) | collective-permute-done | bytes 786464 | tf_op jit(solution)/shard_map/ppermute | solution.py:19
  229.7 4.7 collective-permute-start.4
  234.4 28.0 %collective-permute-done.1 = bf16[1536,256]{1,0:T(8,128)(2,1)S(1)} collective-permute-done((bf16[1536,256]{1,0:T(8,128)(2,1)S(1)}, bf16[1536,256]{1,0:T(8,128)(2,1)S(1)}, u32[]{:S(2)}, u32[]{:S(2)}) %collective-permute-start.1) | collective-permute-done | bytes 786464 | tf_op jit(solution)/shard_map/ppermute | solution.py:19
  264.9 17.5 %collective-permute-start.5 = (bf16[1536,256]{1,0:T(8,128)(2,1)S(1)}, bf16[1536,256]{1,0:T(8,128)(2,1)}, u32[]{:S(2)}, u32[]{:S(2)}) collective-permute-start(bf16[1536,256]{1,0:T(8,128)(2,1)S(1)} %collective-permute-done.4), channel_id=1, source_target_pairs={{0,28},{4,0},{8,4},{12,8},{16,12},{20,16},{24,20},{28,24},{1,29},{... | collective-permute-start | bytes 2359304 | tf_op jit(solution)/shard_map/ppermute | solution.py:21
  282.4 14.3 collective-permute-done.2
  299.4 31.2 %all-gather.1 = bf16[8,1,256]{2,1,0:T(2,128)(2,1)S(1)} all-gather(bf16[1,1,256]{2,1,0:T(2,128)(2,1)S(1)} %reshape.306), channel_id=1, replica_groups=mesh['dp'=8,'mp'=4] {'dp'}, dimensions={0}, use_global_device_ids=true | all-gather | bytes 4608 | tf_op jit(solution)/shard_map/all_gather | solution.py:145
  342.4 4.9 collective-permute-done.6
  359.6 5.7 multiply_reduce_fusion.1
  371.5 87.3 %all-gather.17.cloned.1.call-done = bf16[2048,1536]{1,0:T(8,128)(2,1)} async-done(((bf16[256,1536]{1,0:T(8,128)(2,1)}), bf16[2048,1536]{1,0:T(8,128)(2,1)}) %all-gather.17.cloned.1.call-update) | async-done | bytes 6291472 | tf_op jit(solution)/shard_map/all_gather | solution.py:146
  458.8 11.9 fusion.91
  470.7 88.1 %all-gather.19.cloned.1.call-done = bf16[2048,1536]{1,0:T(8,128)(2,1)} async-done(((bf16[256,1536]{1,0:T(8,128)(2,1)}), bf16[2048,1536]{1,0:T(8,128)(2,1)}) %all-gather.19.cloned.1.call-update) | async-done | bytes 6291472 | tf_op jit(solution)/shard_map/all_gather | solution.py:147
  558.8 11.9 fusion.92
  570.7 16.2 %fusion.20 = (bf16[1024,1536]{1,0:T(8,128)(2,1)}, bf16[1024,1536]{1,0:T(8,128)(2,1)}, bf16[1024,1536]{1,0:T(8,128)(2,1)}) fusion(f32[1024,1536]{1,0:T(8,128)} %fusion.91, f32[1024,1536]{1,0:T(8,128)} %fusion.92, bf16[1024,2048]{1,0:T(8,128)(2,1)S(1)} %copy-done.30, bf16[1536,4096]{1,0:T(8,128)(2,1)} %constant_dynamic-update-slice_fusion, s32[]{:T(128)S(6)} %select_n.52), kind=kOutput, calls=%fused_computation.48 | convolution fusion | flops 6466043904 | bytes 32505860 | tf_op jit(solution)/shard_map/dot_general | solution.py:78
  586.9 10.6 fusion.93
  597.4 10.8 add_convert_fusion.1
  608.4 11.1 fusion.34
  619.4 72.6 %all-reduce.16.cloned.1.call-done = bf16[1024,2048]{1,0:T(8,128)(2,1)} async-done(((bf16[1024,2048]{1,0:T(8,128)(2,1)}), bf16[1024,2048]{1,0:T(8,128)(2,1)}) %all-reduce.16.cloned.1.call-update) | async-done | bytes 4194320 | tf_op jit(solution)/shard_map/psum | solution.py:229
  692.1 6.0 fusion.5
  699.2 5.0 fusion.4
  727.1 4.4 broadcast_multiply_fusion
  737.0 4.7 fusion.44
  742.7 5.7 fusion.94
  758.6 4.9 convolution_convert_fusion.5
  763.8 6.5 convolution_convert_fusion.4
  770.4 7.1 convolution_convert_fusion.3
  777.6 11.6 convolution_convert_fusion.2
  791.0 11.0 convolution_convert_fusion.1
  803.9 10.8 convolution_convert_fusion
  817.8 137.3 %all-reduce.18.cloned.1.call-done = (bf16[1024,2048]{1,0:T(8,128)(2,1)}, bf16[1024,2048]{1,0:T(8,128)(2,1)}) async-done(((bf16[1024,2048]{1,0:T(8,128)(2,1)}, bf16[1024,2048]{1,0:T(8,128)(2,1)}), (bf16[1024,2048]{1,0:T(8,128)(2,1)}, bf16[1024,2048]{1,0:T(8,128)(2,1)})) %all-reduce.18.cloned.1.call-update) | async-done | bytes 8388624 | tf_op jit(solution)/shard_map/psum | solution.py:214
  955.1 6.5 multiply_reduce_fusion
  961.6 22.2 %all-reduce.6 = (bf16[2048]{0:T(1024)(128)(2,1)S(1)}, bf16[128]{0:T(256)(128)(2,1)S(1)}, bf16[128]{0:T(256)(128)(2,1)S(1)}, bf16[2048]{0:T(1024)(128)(2,1)S(1)}) all-reduce(bf16[2048]{0:T(1024)(128)(2,1)S(1)} %get-tuple-element.84, bf16[128]{0:T(256)(128)(2,1)S(1)} %reduce_sum.170, ...), channel_id=2, replica_groups=mesh['dp'=8,'mp'=4] {'dp'}, use_global_device_ids=true, to_apply=%region_21.22.clone | all-reduce | flops 4352 | bytes 17408
  983.9 38.9 %reduce-scatter.12.cloned.1.call-done = bf16[256,256]{1,0:T(8,128)(2,1)} async-done(((bf16[2048,256]{1,0:T(8,128)(2,1)}), bf16[256,256]{1,0:T(8,128)(2,1)}) %reduce-scatter.12.cloned.1.call-update) | async-done | bytes 131088 | tf_op jit(solution)/shard_map/reduce_scatter | solution.py:331
  1024.5 5.6 all-reduce.8
  1030.1 6.6 convert_element_type.272
  1037.7 56.6 %reduce-scatter.8.cloned.1.call-done = bf16[256,512]{1,0:T(8,128)(2,1)} async-done(((bf16[2048,512]{1,0:T(8,128)(2,1)}), bf16[256,512]{1,0:T(8,128)(2,1)}) %reduce-scatter.8.cloned.1.call-update) | async-done | bytes 262160 | tf_op jit(solution)/shard_map/reduce_scatter | solution.py:325
  1096.1 69.5 %reduce-scatter.14.cloned.1.call-done = bf16[512,256]{1,0:T(8,128)(2,1)} async-done(((bf16[512,2048]{1,0:T(8,128)(2,1)}), bf16[512,256]{1,0:T(8,128)(2,1)}) %reduce-scatter.14.cloned.1.call-update) | async-done | bytes 262160 | tf_op jit(solution)/shard_map/reduce_scatter | solution.py:334
  1170.6 6.0 multiply_add_fusion
  1176.6 109.8 %reduce-scatter.16.cloned.1.call-done = bf16[256,1536]{1,0:T(8,128)(2,1)} async-done(((bf16[2048,1536]{1,0:T(8,128)(2,1)}), bf16[256,1536]{1,0:T(8,128)(2,1)}) %reduce-scatter.16.cloned.1.call-update) | async-done | bytes 786448 | tf_op jit(solution)/shard_map/reduce_scatter | solution.py:342
  1288.9 118.6 %reduce-scatter.18.cloned.1.call-done = bf16[256,1536]{1,0:T(8,128)(2,1)} async-done(((bf16[2048,1536]{1,0:T(8,128)(2,1)}), bf16[256,1536]{1,0:T(8,128)(2,1)}) %reduce-scatter.18.cloned.1.call-update) | async-done | bytes 786448 | tf_op jit(solution)/shard_map/reduce_scatter | solution.py:345
  1409.9 119.0 %reduce-scatter.20.cloned.1.call-done = bf16[1536,256]{1,0:T(8,128)(2,1)} async-done(((bf16[1536,2048]{1,0:T(8,128)(2,1)}), bf16[1536,256]{1,0:T(8,128)(2,1)}) %reduce-scatter.20.cloned.1.call-update) | async-done | bytes 786448 | tf_op jit(solution)/shard_map/reduce_scatter | solution.py:348
  (324 shorter events, 137.8 us)
Async XLA Ops:
  7.2 34.9 %copy-start.55 = (u32[32]{0:T(128)S(1)}, u32[32]{0:T(128)}, u32[]{:S(2)}) copy-start(u32[32]{0:T(128)} %constant.135) | copy-start | bytes 388
  7.2 55.8 %copy-start.50 = (s32[1,1024]{1,0:T(1,128)S(1)}, s32[1,1024]{1,0:T(1,128)}, u32[]{:S(2)}) copy-start(s32[1,1024]{1,0:T(1,128)} %param.15) | copy-start | bytes 12292
  7.2 34.8 %copy-start.60 = (f32[16]{0:T(128)S(1)}, f32[16]{0:T(128)}, u32[]{:S(2)}) copy-start(f32[16]{0:T(128)} %param.19) | copy-start | bytes 196
  7.2 34.8 %copy-start.61 = (f32[16]{0:T(128)S(1)}, f32[16]{0:T(128)}, u32[]{:S(2)}) copy-start(f32[16]{0:T(128)} %param.18) | copy-start | bytes 196
  7.2 56.5 %all-gather.11.cloned.1.call-start = ((), (), s32[]{:S(2)}) async-start(), calls=%async_computation.8 | async-start | bytes 1179648 | tf_op jit(solution)/shard_map/all_gather | solution.py:131
  8.9 86.7 %all-gather.9.cloned.1.call-start = ((), (), s32[]{:S(2)}) async-start(), calls=%async_computation.7 | async-start | bytes 1179648 | tf_op jit(solution)/shard_map/all_gather | solution.py:132
  10.6 135.8 %all-gather.13.cloned.1.call-start = ((), (), s32[]{:S(2)}) async-start(), calls=%async_computation.9 | async-start | bytes 2359296 | tf_op jit(solution)/shard_map/all_gather | solution.py:130
  12.5 186.0 %all-gather.15.cloned.1.call-start = ((), (), s32[]{:S(2)}) async-start(), calls=%async_computation.10 | async-start | bytes 2359296 | tf_op jit(solution)/shard_map/all_gather | solution.py:133
  14.3 345.3 %all-reduce.14.cloned.1.call-start = ((), (), s32[]{:S(2)}) async-start(), calls=%async_computation.11 | async-start | bytes 16777216 | tf_op jit(solution)/shard_map/psum | solution.py:203
  38.9 107.5 %copy-start.48 = (f32[8,1,256]{2,1,0:T(1,128)}, f32[8,1,256]{2,1,0:T(1,128)S(1)}, u32[]{:S(2)}) copy-start(f32[8,1,256]{2,1,0:T(1,128)S(1)} %convert_element_type.295) | copy-start | bytes 24580
  42.0 104.4 %copy-start.51 = (f32[1024]{0:T(1024)}, f32[1024]{0:T(1024)S(1)}, u32[]{:S(2)}) copy-start(f32[1024]{0:T(1024)S(1)} %add_rsqrt_fusion.3) | copy-start | bytes 12292
  62.9 89.5 %copy-start.13 = (f32[1024,128]{0,1:T(8,128)}, f32[1024,128]{0,1:T(8,128)S(1)}, u32[]{:S(2)}) copy-start(f32[1024,128]{0,1:T(8,128)S(1)} %pad_maximum_fusion.5) | copy-start | bytes 1572868
  63.0 89.4 %copy-start.9 = (f32[1024,128]{0,1:T(8,128)}, f32[1024,128]{0,1:T(8,128)S(1)}, u32[]{:S(2)}) copy-start(f32[1024,128]{0,1:T(8,128)S(1)} %pad_maximum_fusion.4) | copy-start | bytes 1572868
  69.1 87.5 %copy-start.21 = (bf16[1024,2,128,1]{0,2,3,1:T(8,128)(2,1)}, bf16[1024,2,128,1]{0,2,3,1:T(8,128)(2,1)S(1)}, u32[]{:S(2)}) copy-start(bf16[1024,2,128,1]{0,2,3,1:T(8,128)(2,1)S(1)} %fusion.75) | copy-start | bytes 1572868
  99.6 61.6 %copy-start.36 = (bf16[1024,256]{0,1:T(8,128)(2,1)}, bf16[1024,256]{0,1:T(8,128)(2,1)S(1)}, u32[]{:S(2)}) copy-start(bf16[1024,256]{0,1:T(8,128)(2,1)S(1)} %convolution_convert_fusion.7) | copy-start | bytes 1572868
  163.4 35.0 %copy-start.43 = (bf16[1024,2,2,128]{0,3,2,1:T(8,128)(2,1)}, bf16[1024,2,2,128]{0,3,2,1:T(8,128)(2,1)S(1)}, u32[]{:S(2)}) copy-start(bf16[1024,2,2,128]{0,3,2,1:T(8,128)(2,1)S(1)} %pad_maximum_fusion.3) | copy-start | bytes 3145732
  205.7 93.6 %copy-start.59 = (f32[256]{0:T(256)S(1)}, f32[256]{0:T(256)}, u32[]{:S(2)}) copy-start(f32[256]{0:T(256)} %param.24) | copy-start | bytes 3076
  205.8 253.0 %all-gather.17.cloned.1.call-start = ((), (), s32[]{:S(2)}) async-start(), calls=%async_computation.12 | async-start | bytes 7077888 | tf_op jit(solution)/shard_map/all_gather | solution.py:146
  208.1 350.7 %all-gather.19.cloned.1.call-start = ((), (), s32[]{:S(2)}) async-start(), calls=%async_computation.13 | async-start | bytes 7077888 | tf_op jit(solution)/shard_map/all_gather | solution.py:147
  208.3 21.4 %copy-start.45 = (bf16[1536,256]{1,0:T(8,128)(2,1)}, bf16[1536,256]{1,0:T(8,128)(2,1)S(1)}, u32[]{:S(2)}) copy-start(bf16[1536,256]{1,0:T(8,128)(2,1)S(1)} %convert_element_type.250) | copy-start | bytes 2359300
  208.3 21.4 %collective-permute-start = (bf16[1536,256]{1,0:T(8,128)(2,1)S(1)}, bf16[1536,256]{1,0:T(8,128)(2,1)S(1)}, u32[]{:S(2)}, u32[]{:S(2)}) collective-permute-start(bf16[1536,256]{1,0:T(8,128)(2,1)S(1)} %convert_element_type.250), channel_id=1, source_target_pairs={{0,4},{4,8},{8,12},{12,16},{16,20},{20,24},{24,28},{28,0},{1,5},{5... | collective-permute-start | bytes 2359304 | tf_op jit(solution)/shard_map/ppermute | solution.py:19
  212.3 479.8 %all-reduce.16.cloned.1.call-start = ((), (), s32[]{:S(2)}) async-start(), calls=%async_computation.14 | async-start | bytes 8388608 | tf_op jit(solution)/shard_map/psum | solution.py:229
  229.7 32.7 %collective-permute-start.1 = (bf16[1536,256]{1,0:T(8,128)(2,1)S(1)}, bf16[1536,256]{1,0:T(8,128)(2,1)S(1)}, u32[]{:S(2)}, u32[]{:S(2)}) collective-permute-start(bf16[1536,256]{1,0:T(8,128)(2,1)S(1)} %collective-permute-done), channel_id=1, source_target_pairs={{0,4},{4,8},{8,12},{12,16},{16,20},{20,24},{24,28},{28,0},{1,5},{5... | collective-permute-start | bytes 2359304 | tf_op jit(solution)/shard_map/ppermute | solution.py:19
  229.7 35.2 %collective-permute-start.4 = (bf16[1536,256]{1,0:T(8,128)(2,1)}, bf16[1536,256]{1,0:T(8,128)(2,1)S(1)}, u32[]{:S(2)}, u32[]{:S(2)}) collective-permute-start(bf16[1536,256]{1,0:T(8,128)(2,1)} %copy-done.45), channel_id=1, source_target_pairs={{0,28},{4,0},{8,4},{12,8},{16,12},{20,16},{24,20},{28,24},{1,29},{... | collective-permute-start | bytes 2359304 | tf_op jit(solution)/shard_map/ppermute | solution.py:21
  262.4 34.4 %collective-permute-start.2 = (bf16[1536,256]{1,0:T(8,128)(2,1)S(1)}, bf16[1536,256]{1,0:T(8,128)(2,1)}, u32[]{:S(2)}, u32[]{:S(2)}) collective-permute-start(bf16[1536,256]{1,0:T(8,128)(2,1)S(1)} %collective-permute-done.1), channel_id=1, source_target_pairs={{0,4},{4,8},{8,12},{12,16},{16,20},{20,24},{24,28},{28,0},{1,5},{5... | collective-permute-start | bytes 2359304 | tf_op jit(solution)/shard_map/ppermute | solution.py:19
  264.9 65.7 %collective-permute-start.5 = (bf16[1536,256]{1,0:T(8,128)(2,1)S(1)}, bf16[1536,256]{1,0:T(8,128)(2,1)}, u32[]{:S(2)}, u32[]{:S(2)}) collective-permute-start(bf16[1536,256]{1,0:T(8,128)(2,1)S(1)} %collective-permute-done.4), channel_id=1, source_target_pairs={{0,28},{4,0},{8,4},{12,8},{16,12},{20,16},{24,20},{28,24},{1,29},{... | collective-permute-start | bytes 2359304 | tf_op jit(solution)/shard_map/ppermute | solution.py:21
  296.8 33.9 %collective-permute-start.3 = (bf16[1536,256]{1,0:T(8,128)(2,1)}, bf16[1536,256]{1,0:T(8,128)(2,1)}, u32[]{:S(2)}, u32[]{:S(2)}) collective-permute-start(bf16[1536,256]{1,0:T(8,128)(2,1)} %collective-permute-done.2), channel_id=1, source_target_pairs={{0,4},{4,8},{8,12},{12,16},{16,20},{20,24},{24,28},{28,0},{1,5},{5... | collective-permute-start | bytes 2359304 | tf_op jit(solution)/shard_map/ppermute | solution.py:19
  330.6 16.7 %collective-permute-start.6 = (bf16[1536,256]{1,0:T(8,128)(2,1)}, bf16[1536,256]{1,0:T(8,128)(2,1)S(1)}, u32[]{:S(2)}, u32[]{:S(2)}) collective-permute-start(bf16[1536,256]{1,0:T(8,128)(2,1)} %collective-permute-done.5), channel_id=1, source_target_pairs={{0,28},{4,0},{8,4},{12,8},{16,12},{20,16},{24,20},{28,24},{1,29},{... | collective-permute-start | bytes 2359304 | tf_op jit(solution)/shard_map/ppermute | solution.py:21
  335.0 17.5 %copy-start.33 = (bf16[1536,256]{1,0:T(8,128)(2,1)S(1)}, bf16[1536,256]{1,0:T(8,128)(2,1)}, u32[]{:S(2)}) copy-start(bf16[1536,256]{1,0:T(8,128)(2,1)} %copy-done.32) | copy-start | bytes 2359300
  558.8 11.9 copy-start.30
  558.8 28.1 %slice-start.10 = ((s8[6291456]{0:T(1024)(128)(4,1)}), s8[4194304]{0:T(1024)(128)(4,1)S(1)}, s32[]{:S(2)}) async-start(s8[6291456]{0:T(1024)(128)(4,1)} %bitcast.281), calls=%async_computation.33 | async-start | bytes 8388608
  570.7 16.2 %slice-start.11 = ((s8[6291456]{0:T(1024)(128)(4,1)}), s8[2097152]{0:T(1024)(128)(4,1)S(1)}, s32[]{:S(2)}) async-start(s8[6291456]{0:T(1024)(128)(4,1)} %bitcast.281), calls=%async_computation.34 | async-start | bytes 4194304
  586.9 10.6 copy-start.56
  586.9 10.6 copy-start.63
  608.2 207.9 %reduce-scatter.10.cloned.1.call-start = ((), (), s32[]{:S(2)}) async-start(), calls=%async_computation.16 | async-start | bytes 1179648 | tf_op jit(solution)/shard_map/reduce_scatter | solution.py:328
  692.1 15.5 %slice-start = ((s8[8388608]{0:T(1024)(128)(4,1)}), s8[4194304]{0:T(1024)(128)(4,1)S(1)}, s32[]{:S(2)}) async-start(s8[8388608]{0:T(1024)(128)(4,1)} %bitcast.227), calls=%async_computation.23 | async-start | bytes 8388608
  699.1 8.4 slice-start.1
  707.6 7.7 copy-start.26
  707.6 7.6 slice-start.4
  712.8 10.9 copy-start.17
  736.8 218.3 %all-reduce.18.cloned.1.call-start = ((), (), s32[]{:S(2)}) async-start(), calls=%async_computation.22 | async-start | bytes 16777216 | tf_op jit(solution)/shard_map/psum | solution.py:214
  742.7 9.6 slice-start.2
  758.5 264.3 %reduce-scatter.12.cloned.1.call-start = ((), (), s32[]{:S(2)}) async-start(), calls=%async_computation.17 | async-start | bytes 1179648 | tf_op jit(solution)/shard_map/reduce_scatter | solution.py:331
  763.5 330.8 %reduce-scatter.8.cloned.1.call-start = ((), (), s32[]{:S(2)}) async-start(), calls=%async_computation.15 | async-start | bytes 2359296 | tf_op jit(solution)/shard_map/reduce_scatter | solution.py:325
  770.3 395.4 %reduce-scatter.14.cloned.1.call-start = ((), (), s32[]{:S(2)}) async-start(), calls=%async_computation.18 | async-start | bytes 2359296 | tf_op jit(solution)/shard_map/reduce_scatter | solution.py:334
  777.5 508.9 %reduce-scatter.16.cloned.1.call-start = ((), (), s32[]{:S(2)}) async-start(), calls=%async_computation.19 | async-start | bytes 7077888 | tf_op jit(solution)/shard_map/reduce_scatter | solution.py:342
  789.1 618.3 %reduce-scatter.18.cloned.1.call-start = ((), (), s32[]{:S(2)}) async-start(), calls=%async_computation.20 | async-start | bytes 7077888 | tf_op jit(solution)/shard_map/reduce_scatter | solution.py:345
  802.0 726.9 %reduce-scatter.20.cloned.1.call-start = ((), (), s32[]{:S(2)}) async-start(), calls=%async_computation.21 | async-start | bytes 7077888 | tf_op jit(solution)/shard_map/reduce_scatter | solution.py:348
  (52 other events, 178.1 us)
Sparse Core Ops, SparseCore 0:
  10.8 42.9 all-gather.10
  56.4 39.1 all-gather.8
  98.3 48.0 all-gather.12
  148.9 49.5 all-gather.14
  205.9 151.0 all-reduce.13
  359.6 99.1 all-gather.16
  461.5 97.1 all-gather.18
  608.4 83.6 all-reduce.15
  736.9 63.4 reduce-scatter.9
  802.8 152.2 all-reduce.17
  959.1 63.7 reduce-scatter.11
  1027.2 67.0 reduce-scatter.7
  1098.3 67.3 reduce-scatter.13
  1169.5 116.8 reduce-scatter.15
  1290.3 117.1 reduce-scatter.17
  1411.3 117.4 reduce-scatter.19
